TPU v7x, 128 devices: a whole 4x4x4 slice. The times are simulated.
128 devices in a mesh: dp: 32 (over z, x, core), seq: 4 (over y).
Axes of the slice: x: 4, y: 4, z: 4, core: 2. Of those that a mesh axis runs over, the one named last changes fastest.
Arguments:
- queries: bfloat16 [32768, 2560], P(('dp', 'seq')), may hold values from -200 to 200
- keys: bfloat16 [32768, 2560], P(('dp', 'seq')), may hold values from -200 to 200
- values: bfloat16 [32768, 2560], P(('dp', 'seq')), may hold values from -6 to 6
- gain_q: float32 [2560], replicated, may hold values from 0.5 to 1.5
- gain_k: float32 [2560], replicated, may hold values from 0.5 to 1.5
- tile_pairs: int32 [16, 8], replicated, may hold values from 0 to 15, as said below
- tile_lens: int32 [32, 16], P('dp'), may hold values from 40 to 64
- out_grad: bfloat16 [32768, 5120], P(('dp', 'seq')), may hold values from -24 to 24
- w_out: bfloat16 [5120, 2560], P('dp', 'seq'), may hold values from -0.125 to 0.125
Outputs:
- grad_q: bfloat16 [32768, 2560], P(('dp', 'seq'))
- grad_k: bfloat16 [32768, 2560], P(('dp', 'seq'))
- grad_v: bfloat16 [32768, 2560], P(('dp', 'seq'))
- grad_w: float32 [5120, 2560], P('dp', 'seq')
Inputs may be any that keep to these rules, and one draw needn't show every extreme that they name: `tile_pairs`: row a lists 8 different tiles of the window, with tile a first.
All inputs are finite; a program needn't handle non-finite values.
Results may differ from a plain program's by a relative error of at most 0.02.
Values may be sent and summed in bfloat16 or wider, within the bound.
No kernel may reach another device: no remote copies, remote signals or barrier semaphores. Data moves between devices by JAX's collectives and lax.ppermute only.
A program may use at most 128 MiB of HBM per device.

v0:
```python
import math
import jax
import jax.numpy as jnp
from jax import lax
from jax.sharding import PartitionSpec as P

HEAD_DIM = 128
EPS = 1e-06


def multiply(pattern, left, right):
    return jnp.einsum(pattern, left, right, preferred_element_type=jnp.float32)


def normalize(field, gain):
    values_f = field.astype(jnp.float32)
    row_scale = lax.rsqrt(jnp.mean(values_f * values_f, axis=-1, keepdims=True) + EPS)
    return ((values_f * row_scale * gain).astype(jnp.bfloat16), row_scale)


def norm_finish(values_f, row_scale, gated, inner, width):
    return (row_scale * gated - values_f * row_scale**3 * inner / width).astype(jnp.bfloat16)


def tile_attention(query_tiles, key_tiles, value_tiles, grad_tiles, tile_pairs, live_lengths):
    tile_count, tile_rows, head_width = query_tiles.shape
    neighbours = tile_pairs.shape[1]
    factor = 1.0 / math.sqrt(head_width)
    key_near = jnp.take(key_tiles, tile_pairs, axis=0).reshape(
        tile_count, neighbours * tile_rows, head_width
    )
    value_near = jnp.take(value_tiles, tile_pairs, axis=0).reshape(
        tile_count, neighbours * tile_rows, head_width
    )
    near_lengths = jnp.take(live_lengths, tile_pairs, axis=0)
    live = (
        jnp.arange(tile_rows, dtype=jnp.int32)[None, None, :] < near_lengths[:, :, None]
    ).reshape(tile_count, neighbours * tile_rows)
    scores = multiply("aqd,akd->aqk", query_tiles, key_near) * factor
    scores = jnp.where(live[:, None, :], scores, -jnp.inf)
    row_max = jnp.max(scores, axis=-1, keepdims=True)
    weights = jnp.exp(scores - row_max)
    probs = weights / jnp.sum(weights, axis=-1, keepdims=True)
    probs_low = probs.astype(jnp.bfloat16)
    attended = multiply("aqk,akd->aqd", probs_low, value_near).astype(jnp.bfloat16)
    grad_probs = multiply("aqd,akd->aqk", grad_tiles, value_near)
    delta = jnp.sum(probs * grad_probs, axis=-1, keepdims=True)
    grad_scores = (probs * (grad_probs - delta)).astype(jnp.bfloat16)
    grad_query = (multiply("aqk,akd->aqd", grad_scores, key_near) * factor).astype(jnp.bfloat16)
    grad_key_near = multiply("aqk,aqd->akd", grad_scores, query_tiles) * factor
    grad_value_near = multiply("aqk,aqd->akd", probs_low, grad_tiles)
    owners = (
        tile_pairs[:, :, None] == jnp.arange(tile_count, dtype=jnp.int32)[None, None, :]
    ).astype(jnp.float32)
    grad_key = jnp.einsum(
        "anb,antd->btd",
        owners,
        grad_key_near.reshape(tile_count, neighbours, tile_rows, head_width),
        precision=lax.Precision.HIGHEST,
    ).astype(jnp.bfloat16)
    grad_value = jnp.einsum(
        "anb,antd->btd",
        owners,
        grad_value_near.reshape(tile_count, neighbours, tile_rows, head_width),
        precision=lax.Precision.HIGHEST,
    ).astype(jnp.bfloat16)
    return (attended, grad_query, grad_key, grad_value)


def per_device(queries, keys, values, gain_q, gain_k, tile_pairs, tile_lens, out_grad, w_out):
    seq_count = lax.axis_size("seq")
    dp_count = lax.axis_size("dp")
    tok_rows = queries.shape[0]
    width = queries.shape[1]
    local_width = width // seq_count
    clip_rows = tok_rows * seq_count
    tile_count = tile_pairs.shape[0]
    tile_rows = clip_rows // tile_count
    head_count = local_width // HEAD_DIM
    clip_lengths = tile_lens[0]
    query_normed, query_scale = normalize(queries, gain_q)
    key_normed, key_scale = normalize(keys, gain_k)
    query_heads, key_heads, value_heads = (
        lax.all_to_all(query_normed, "seq", split_axis=1, concat_axis=0, tiled=True),
        lax.all_to_all(key_normed, "seq", split_axis=1, concat_axis=0, tiled=True),
        lax.all_to_all(values, "seq", split_axis=1, concat_axis=0, tiled=True),
    )
    cot_all = lax.all_gather(out_grad, "seq", axis=0, tiled=True)
    columns = cot_all
    grad_attended = jnp.dot(
        columns, lax.all_gather(w_out, "dp", axis=0, tiled=True), preferred_element_type=jnp.float32
    ).astype(jnp.bfloat16)

    def split(field):
        return field.reshape(tile_count, tile_rows, head_count, HEAD_DIM).transpose(2, 0, 1, 3)

    def merge(field):
        return field.transpose(1, 2, 0, 3).reshape(clip_rows, local_width)

    def one_head(group):
        return tile_attention(group[0], group[1], group[2], group[3], tile_pairs, clip_lengths)

    attended, grad_qn, grad_kn, grad_vh = lax.map(
        one_head, (split(query_heads), split(key_heads), split(value_heads), split(grad_attended))
    )
    attended = merge(attended)
    grad_qn = merge(grad_qn)
    grad_kn = merge(grad_kn)
    grad_vh = merge(grad_vh)
    columns = cot_all
    grad_w = lax.psum_scatter(
        (
            jnp.einsum("td,te->de", columns, attended, preferred_element_type=jnp.float32)
            / dp_count
        ).astype(jnp.bfloat16),
        "dp",
        scatter_dimension=0,
        tiled=True,
    ).astype(jnp.float32)
    grad_qt, grad_kt, grad_v = (
        lax.all_to_all(grad_qn, "seq", split_axis=0, concat_axis=1, tiled=True),
        lax.all_to_all(grad_kn, "seq", split_axis=0, concat_axis=1, tiled=True),
        lax.all_to_all(grad_vh, "seq", split_axis=0, concat_axis=1, tiled=True),
    )
    query_full = queries.astype(jnp.float32)
    key_full = keys.astype(jnp.float32)
    gated_q = gain_q * grad_qt.astype(jnp.float32)
    gated_k = gain_k * grad_kt.astype(jnp.float32)
    inner_q = jnp.sum(gated_q * query_full, axis=-1, keepdims=True)
    inner_k = jnp.sum(gated_k * key_full, axis=-1, keepdims=True)
    grad_q = norm_finish(query_full, query_scale, gated_q, inner_q, width)
    grad_k = norm_finish(key_full, key_scale, gated_k, inner_k, width)
    return (grad_q, grad_k, grad_v, grad_w)


def solution(mesh):
    return jax.shard_map(
        per_device,
        mesh=mesh,
        in_specs=(
            P(("dp", "seq"), None),
            P(("dp", "seq"), None),
            P(("dp", "seq"), None),
            P(),
            P(),
            P(),
            P("dp", None),
            P(("dp", "seq"), None),
            P("dp", "seq"),
        ),
        out_specs=(
            P(("dp", "seq"), None),
            P(("dp", "seq"), None),
            P(("dp", "seq"), None),
            P("dp", "seq"),
        ),
        check_vma=False,
    )
```

profile of v0, /device:TPU:0, one launch (start us, length us, event | category | flops | bytes accessed | tf_op | source)
XLA Modules:
  0.0 484.7 jit_solution(18076181013758219229)
XLA Ops:
  12.3 4.5 all-to-all-start
  20.8 2.4 copy.75
  23.3 11.4 %all-to-all-done = bf16[256,4,640]{2,0,1:T(8,128)(2,1)S(1)} async-done(((bf16[256,4,640]{2,0,1:T(8,128)(2,1)}), bf16[256,4,640]{2,0,1:T(8,128)(2,1)S(1)}, u32[]{:S(2)}, u32[]{:S(2)}) %all-to-all-start) | async-done | bytes 1310752 | tf_op jit(solution)/shard_map/all_to_all | solution.py:84
  34.7 3.5 all-to-all-start.1
  38.3 2.5 copy.126
  40.8 14.4 %all-to-all-done.1 = bf16[256,4,640]{2,0,1:T(8,128)(2,1)S(1)} async-done(((bf16[256,4,640]{2,0,1:T(8,128)(2,1)}), bf16[256,4,640]{2,0,1:T(8,128)(2,1)S(1)}, u32[]{:S(2)}, u32[]{:S(2)}) %all-to-all-start.1) | async-done | bytes 1310752 | tf_op jit(solution)/shard_map/all_to_all | solution.py:85
  55.2 4.3 all-to-all-start.2
  63.1 3.1 reshape.159
  67.6 8.1 %all-to-all-done.2 = bf16[256,4,640]{2,0,1:T(8,128)(2,1)} async-done(((bf16[256,4,640]{2,0,1:T(8,128)(2,1)}), bf16[256,4,640]{2,0,1:T(8,128)(2,1)}, u32[]{:S(2)}, u32[]{:S(2)}) %all-to-all-start.2) | async-done | bytes 1310752 | tf_op jit(solution)/shard_map/all_to_all | solution.py:86
  75.7 3.2 reshape.160
  80.3 83.5 %all-gather.3.cloned.1.call-done = bf16[1024,5120]{1,0:T(8,128)(2,1)} async-done(((bf16[256,5120]{1,0:T(8,128)(2,1)}), bf16[1024,5120]{1,0:T(8,128)(2,1)}) %all-gather.3.cloned.1.call-update) | async-done | bytes 10485776 | tf_op jit(solution)/shard_map/all_gather | solution.py:88
  163.8 13.7 %convolution_convert_fusion.1 = bf16[1024,640]{1,0:T(8,128)(2,1)} fusion(bf16[1024,5120]{1,0:T(8,128)(2,1)} %all-gather.3.cloned.1.call-done, bf16[5120,640]{1,0:T(8,128)(2,1)} %all-gather.5.cloned.1.call-done), kind=kOutput, calls=%fused_computation.95 | convolution fusion | flops 6711541760 | bytes 18350080 | tf_op jit(solution)/shard_map/dot_general | solution.py:90
  177.5 3.1 reshape.161
  182.1 182.6 %while.18 = (s32[]{:T(128)}, bf16[5,16,64,128]{3,2,1,0:T(8,128)(2,1)}, bf16[5,16,64,128]{3,2,1,0:T(8,128)(2,1)}, bf16[5,16,64,128]{3,1,2,0:T(8,128)(2,1)}, bf16[...) while((s32[]{:T(128)}, ...), condition=%wide.region_6.8_spmd, body=%wide.region_2.7_spmd.sunk | while | flops 1219638656 | bytes 88276472 | solution.py:103
  187.9 4.0 broadcast_select_fusion.6
  194.5 3.6 fusion.136
  201.7 2.8 convolution_multiply_fusion.3
  204.6 7.3 %fusion.138 = bf16[5,16,64,128]{3,1,2,0:T(8,128)(2,1)} fusion(bf16[5,16,64,128]{3,1,2,0:T(8,128)(2,1)} %get-tuple-element.341, s32[]{:T(128)S(6)} %copy.142, f32[16,8,64,128]{3,2,1,0:T(8,128)} %bitcast.172, s32[16,8]{0,1:T(8,128)S(1)} %copy.132), kind=kOutput, calls=%fused_computation.26.clone.1 | convolution fusion | flops 201459712 | bytes 4456964 | tf_op jit(solution)/shard_map/while/body/eval_jaxpr/anb,antd->btd/dot_general | solution.py:55
  213.8 5.1 %fusion.140 = bf16[5,16,64,128]{3,1,2,0:T(8,128)(2,1)} fusion(bf16[5,16,64,128]{3,1,2,0:T(8,128)(2,1)} %get-tuple-element.342, s32[]{:T(128)S(6)} %copy.142, f32[16,8,64,128]{3,2,1,0:T(8,128)S(1)} %bitcast.177, s32[16,8]{0,1:T(8,128)S(1)} %copy.132), kind=kOutput, calls=%fused_computation.28.clone.1 | convolution fusion | flops 201459712 | bytes 4456964 | tf_op jit(solution)/shard_map/while/body/eval_jaxpr/anb,antd->btd/dot_general | solution.py:61
  224.3 4.0 broadcast_select_fusion.6
  228.6 2.3 fusion.135
  230.9 3.6 fusion.136
  238.0 2.8 convolution_multiply_fusion.3
  240.9 7.3 %fusion.138 = bf16[5,16,64,128]{3,1,2,0:T(8,128)(2,1)} fusion(bf16[5,16,64,128]{3,1,2,0:T(8,128)(2,1)} %get-tuple-element.341, s32[]{:T(128)S(6)} %copy.142, f32[16,8,64,128]{3,2,1,0:T(8,128)} %bitcast.172, s32[16,8]{0,1:T(8,128)S(1)} %copy.132), kind=kOutput, calls=%fused_computation.26.clone.1 | convolution fusion | flops 201459712 | bytes 4456964 | tf_op jit(solution)/shard_map/while/body/eval_jaxpr/anb,antd->btd/dot_general | solution.py:55
  250.1 5.1 %fusion.140 = bf16[5,16,64,128]{3,1,2,0:T(8,128)(2,1)} fusion(bf16[5,16,64,128]{3,1,2,0:T(8,128)(2,1)} %get-tuple-element.342, s32[]{:T(128)S(6)} %copy.142, f32[16,8,64,128]{3,2,1,0:T(8,128)S(1)} %bitcast.177, s32[16,8]{0,1:T(8,128)S(1)} %copy.132), kind=kOutput, calls=%fused_computation.28.clone.1 | convolution fusion | flops 201459712 | bytes 4456964 | tf_op jit(solution)/shard_map/while/body/eval_jaxpr/anb,antd->btd/dot_general | solution.py:61
  260.7 4.0 broadcast_select_fusion.6
  267.3 3.6 fusion.136
  274.4 2.8 convolution_multiply_fusion.3
  277.3 7.2 %fusion.138 = bf16[5,16,64,128]{3,1,2,0:T(8,128)(2,1)} fusion(bf16[5,16,64,128]{3,1,2,0:T(8,128)(2,1)} %get-tuple-element.341, s32[]{:T(128)S(6)} %copy.142, f32[16,8,64,128]{3,2,1,0:T(8,128)} %bitcast.172, s32[16,8]{0,1:T(8,128)S(1)} %copy.132), kind=kOutput, calls=%fused_computation.26.clone.1 | convolution fusion | flops 201459712 | bytes 4456964 | tf_op jit(solution)/shard_map/while/body/eval_jaxpr/anb,antd->btd/dot_general | solution.py:55
  286.5 5.1 %fusion.140 = bf16[5,16,64,128]{3,1,2,0:T(8,128)(2,1)} fusion(bf16[5,16,64,128]{3,1,2,0:T(8,128)(2,1)} %get-tuple-element.342, s32[]{:T(128)S(6)} %copy.142, f32[16,8,64,128]{3,2,1,0:T(8,128)S(1)} %bitcast.177, s32[16,8]{0,1:T(8,128)S(1)} %copy.132), kind=kOutput, calls=%fused_computation.28.clone.1 | convolution fusion | flops 201459712 | bytes 4456964 | tf_op jit(solution)/shard_map/while/body/eval_jaxpr/anb,antd->btd/dot_general | solution.py:61
  297.1 4.0 broadcast_select_fusion.6
  303.6 3.6 fusion.136
  310.8 2.8 convolution_multiply_fusion.3
  313.7 7.3 %fusion.138 = bf16[5,16,64,128]{3,1,2,0:T(8,128)(2,1)} fusion(bf16[5,16,64,128]{3,1,2,0:T(8,128)(2,1)} %get-tuple-element.341, s32[]{:T(128)S(6)} %copy.142, f32[16,8,64,128]{3,2,1,0:T(8,128)} %bitcast.172, s32[16,8]{0,1:T(8,128)S(1)} %copy.132), kind=kOutput, calls=%fused_computation.26.clone.1 | convolution fusion | flops 201459712 | bytes 4456964 | tf_op jit(solution)/shard_map/while/body/eval_jaxpr/anb,antd->btd/dot_general | solution.py:55
  322.9 5.2 %fusion.140 = bf16[5,16,64,128]{3,1,2,0:T(8,128)(2,1)} fusion(bf16[5,16,64,128]{3,1,2,0:T(8,128)(2,1)} %get-tuple-element.342, s32[]{:T(128)S(6)} %copy.142, f32[16,8,64,128]{3,2,1,0:T(8,128)S(1)} %bitcast.177, s32[16,8]{0,1:T(8,128)S(1)} %copy.132), kind=kOutput, calls=%fused_computation.28.clone.1 | convolution fusion | flops 201459712 | bytes 4456964 | tf_op jit(solution)/shard_map/while/body/eval_jaxpr/anb,antd->btd/dot_general | solution.py:61
  333.5 4.0 broadcast_select_fusion.6
  337.8 2.3 fusion.135
  340.1 3.6 fusion.136
  347.2 2.8 convolution_multiply_fusion.3
  350.1 7.3 %fusion.138 = bf16[5,16,64,128]{3,1,2,0:T(8,128)(2,1)} fusion(bf16[5,16,64,128]{3,1,2,0:T(8,128)(2,1)} %get-tuple-element.341, s32[]{:T(128)S(6)} %copy.142, f32[16,8,64,128]{3,2,1,0:T(8,128)} %bitcast.172, s32[16,8]{0,1:T(8,128)S(1)} %copy.132), kind=kOutput, calls=%fused_computation.26.clone.1 | convolution fusion | flops 201459712 | bytes 4456964 | tf_op jit(solution)/shard_map/while/body/eval_jaxpr/anb,antd->btd/dot_general | solution.py:55
  359.3 5.2 %fusion.140 = bf16[5,16,64,128]{3,1,2,0:T(8,128)(2,1)} fusion(bf16[5,16,64,128]{3,1,2,0:T(8,128)(2,1)} %get-tuple-element.342, s32[]{:T(128)S(6)} %copy.142, f32[16,8,64,128]{3,2,1,0:T(8,128)S(1)} %bitcast.177, s32[16,8]{0,1:T(8,128)S(1)} %copy.132), kind=kOutput, calls=%fused_computation.28.clone.1 | convolution fusion | flops 201459712 | bytes 4456964 | tf_op jit(solution)/shard_map/while/body/eval_jaxpr/anb,antd->btd/dot_general | solution.py:61
  364.6 2.4 copy.90
  367.0 11.5 %fusion.68 = bf16[5120,640]{0,1:T(8,128)(2,1)} fusion(bf16[1024,5120]{1,0:T(8,128)(2,1)} %all-gather.3.cloned.1.call-done, bf16[128,8,5,128]{3,2,1,0:T(8,128)(2,1)S(1)} %bitcast.191), kind=kOutput, calls=%fused_computation.66 | convolution fusion | flops 6717440000 | bytes 18350080 | tf_op jit(solution)/shard_map/td,te->de/dot_general | solution.py:113
  378.5 9.5 %copy.97 = bf16[5120,640]{1,0:T(8,128)(2,1)} copy(bf16[5120,640]{0,1:T(8,128)(2,1)} %fusion.68) | data formatting | bytes 13107200
  390.4 2.4 all_to_all.79
  392.8 4.0 all-to-all-start.3
  396.8 2.3 copy.86
  399.1 2.4 all_to_all.81
  401.5 2.3 copy.88
  403.8 2.5 all_to_all.83
  406.2 8.4 %all-to-all-done.3 = bf16[4,256,640]{2,1,0:T(8,128)(2,1)S(1)} async-done(((bf16[4,256,640]{2,1,0:T(8,128)(2,1)}), bf16[4,256,640]{2,1,0:T(8,128)(2,1)S(1)}, u32[]{:S(2)}, u32[]{:S(2)}) %all-to-all-start.3) | async-done | bytes 1310752 | tf_op jit(solution)/shard_map/all_to_all | solution.py:121
  415.7 3.8 all-to-all-start.4
  419.5 3.1 convert_bitcast_fusion.1
  422.6 3.4 copy.85
  426.0 2.4 fusion.76
  430.3 2.4 copy.91
  432.7 3.7 all-to-all-done.4
  437.5 3.5 all-to-all-start.5
  441.0 2.9 convert_bitcast_fusion
  444.0 3.4 copy.87
  447.4 2.4 fusion.84
  451.8 2.4 copy.92
  454.2 2.9 all-to-all-done.5
  459.3 16.6 %reduce-scatter.4.cloned.1.call-done = bf16[160,640]{1,0:T(8,128)(2,1)} async-done(((bf16[5120,640]{1,0:T(8,128)(2,1)}), bf16[160,640]{1,0:T(8,128)(2,1)}) %reduce-scatter.4.cloned.1.call-update) | async-done | bytes 204816
  (200 shorter events, 92.1 us)
Async XLA Ops:
  7.2 52.7 %copy-start = (s32[1,16]{1,0:T(1,128)S(1)}, s32[1,16]{1,0:T(1,128)}, u32[]{:S(2)}) copy-start(s32[1,16]{1,0:T(1,128)} %param.19) | copy-start | bytes 196
  7.2 1.5 copy-start.14
  7.2 73.1 %all-gather.5.cloned.1.call-start = ((), (), s32[]{:S(2)}) async-start(), calls=%async_computation.8 | async-start | bytes 6758400 | tf_op jit(solution)/shard_map/all_gather | solution.py:91
  7.9 155.8 %all-gather.3.cloned.1.call-start = ((), (), s32[]{:S(2)}) async-start(), calls=%async_computation.7 | async-start | bytes 13107200 | tf_op jit(solution)/shard_map/all_gather | solution.py:88
  8.7 1.6 copy-start.16
  9.3 3.0 copy-start.7
  10.3 0.5 copy-start.23
  12.3 22.5 %all-to-all-start = ((bf16[256,4,640]{2,0,1:T(8,128)(2,1)}), bf16[256,4,640]{2,0,1:T(8,128)(2,1)S(1)}, u32[]{:S(2)}, u32[]{:S(2)}) async-start(bf16[256,4,640]{2,0,1:T(8,128)(2,1)} %copy.73), calls=%async_computation | async-start | bytes 2621440 | tf_op jit(solution)/shard_map/all_to_all | solution.py:84
  16.8 2.6 copy-start.18
  18.4 4.9 %copy-start.5 = (bf16[256,2560]{0,1:T(8,128)(2,1)}, bf16[256,2560]{0,1:T(8,128)(2,1)S(1)}, u32[]{:S(2)}) copy-start(bf16[256,2560]{0,1:T(8,128)(2,1)S(1)} %copy.74) | copy-start | bytes 3932164
  19.4 3.9 copy-start.21
  34.7 20.5 %all-to-all-start.1 = ((bf16[256,4,640]{2,0,1:T(8,128)(2,1)}), bf16[256,4,640]{2,0,1:T(8,128)(2,1)S(1)}, u32[]{:S(2)}, u32[]{:S(2)}) async-start(bf16[256,4,640]{2,0,1:T(8,128)(2,1)} %copy.75), calls=%async_computation.1 | async-start | bytes 2621440 | tf_op jit(solution)/shard_map/all_to_all | solution.py:85
  38.3 21.4 %copy-start.20 = (s32[16,8]{0,1:T(8,128)S(1)}, s32[16,8]{0,1:T(8,128)}, u32[]{:S(2)}) copy-start(s32[16,8]{0,1:T(8,128)} %param.18) | copy-start | bytes 1540
  55.2 5.9 %copy-start.11 = (bf16[256,4,640]{2,0,1:T(8,128)(2,1)}, bf16[256,4,640]{2,0,1:T(8,128)(2,1)S(1)}, u32[]{:S(2)}) copy-start(bf16[256,4,640]{2,0,1:T(8,128)(2,1)S(1)} %all-to-all-done.1) | copy-start | bytes 3932164
  55.2 20.5 %all-to-all-start.2 = ((bf16[256,4,640]{2,0,1:T(8,128)(2,1)}), bf16[256,4,640]{2,0,1:T(8,128)(2,1)}, u32[]{:S(2)}, u32[]{:S(2)}) async-start(bf16[256,4,640]{2,0,1:T(8,128)(2,1)} %bitcast.186), calls=%async_computation.2 | async-start | bytes 2621440 | tf_op jit(solution)/shard_map/all_to_all | solution.py:86
  59.6 416.4 %reduce-scatter.4.cloned.1.call-start = ((), (), s32[]{:S(2)}) async-start(), calls=%async_computation.9 | async-start | bytes 6758400
  194.5 3.6 copy-start.2
  194.5 3.6 copy-start.3
  204.6 7.3 %copy-start.4 = (f32[16,64,512]{2,1,0:T(8,128)S(1)}, f32[16,64,512]{2,1,0:T(8,128)}, u32[]{:S(2)}) copy-start(f32[16,64,512]{2,1,0:T(8,128)} %get-tuple-element.322) | copy-start | bytes 6291460 | tf_op jit(solution)/shard_map/while
  230.9 3.6 copy-start.2
  230.9 3.6 copy-start.3
  240.9 7.3 %copy-start.4 = (f32[16,64,512]{2,1,0:T(8,128)S(1)}, f32[16,64,512]{2,1,0:T(8,128)}, u32[]{:S(2)}) copy-start(f32[16,64,512]{2,1,0:T(8,128)} %get-tuple-element.322) | copy-start | bytes 6291460 | tf_op jit(solution)/shard_map/while
  267.3 3.6 copy-start.2
  267.3 3.6 copy-start.3
  277.3 7.3 %copy-start.4 = (f32[16,64,512]{2,1,0:T(8,128)S(1)}, f32[16,64,512]{2,1,0:T(8,128)}, u32[]{:S(2)}) copy-start(f32[16,64,512]{2,1,0:T(8,128)} %get-tuple-element.322) | copy-start | bytes 6291460 | tf_op jit(solution)/shard_map/while
  303.6 3.6 copy-start.2
  303.6 3.6 copy-start.3
  313.7 7.3 %copy-start.4 = (f32[16,64,512]{2,1,0:T(8,128)S(1)}, f32[16,64,512]{2,1,0:T(8,128)}, u32[]{:S(2)}) copy-start(f32[16,64,512]{2,1,0:T(8,128)} %get-tuple-element.322) | copy-start | bytes 6291460 | tf_op jit(solution)/shard_map/while
  340.1 3.6 copy-start.2
  340.1 3.6 copy-start.3
  350.1 7.3 %copy-start.4 = (f32[16,64,512]{2,1,0:T(8,128)S(1)}, f32[16,64,512]{2,1,0:T(8,128)}, u32[]{:S(2)}) copy-start(f32[16,64,512]{2,1,0:T(8,128)} %get-tuple-element.322) | copy-start | bytes 6291460 | tf_op jit(solution)/shard_map/while
  388.0 1.3 copy-start.15
  392.8 21.9 %all-to-all-start.3 = ((bf16[4,256,640]{2,1,0:T(8,128)(2,1)}), bf16[4,256,640]{2,1,0:T(8,128)(2,1)S(1)}, u32[]{:S(2)}, u32[]{:S(2)}) async-start(bf16[4,256,640]{2,1,0:T(8,128)(2,1)} %all_to_all.79), calls=%async_computation.3 | async-start | bytes 2621440 | tf_op jit(solution)/shard_map/all_to_all | solution.py:121
  414.7 1.1 copy-start.13
  415.7 20.7 %all-to-all-start.4 = ((bf16[4,256,640]{2,1,0:T(8,128)(2,1)}), bf16[4,256,640]{2,1,0:T(8,128)(2,1)S(1)}, u32[]{:S(2)}, u32[]{:S(2)}) async-start(bf16[4,256,640]{2,1,0:T(8,128)(2,1)} %all_to_all.81), calls=%async_computation.4 | async-start | bytes 2621440 | tf_op jit(solution)/shard_map/all_to_all | solution.py:122
  422.6 3.4 copy-start.8
  422.6 3.4 copy-start.17
  426.0 2.5 copy-start.9
  426.0 2.5 copy-start.24
  426.0 2.5 copy-start.26
  436.4 1.1 copy-start.12
  437.5 19.6 %all-to-all-start.5 = ((bf16[4,256,640]{2,1,0:T(8,128)(2,1)}), bf16[4,256,640]{2,1,0:T(8,128)(2,1)S(1)}, u32[]{:S(2)}, u32[]{:S(2)}) async-start(bf16[4,256,640]{2,1,0:T(8,128)(2,1)} %all_to_all.83), calls=%async_computation.5 | async-start | bytes 2621440 | tf_op jit(solution)/shard_map/all_to_all | solution.py:123
  444.0 3.4 copy-start.6
  444.0 3.4 copy-start.19
  447.4 2.6 copy-start.10
  447.4 2.6 copy-start.22
  447.4 2.6 copy-start.25
  457.1 20.8 %copy-start.1 = (s32[1,16]{1,0:T(1,128)S(1)}, s32[1,16]{1,0:T(1,128)}, u32[]{:S(2)}) copy-start(s32[1,16]{1,0:T(1,128)} %param.19) | copy-start | bytes 196
Sparse Core Ops, SparseCore 0:
  10.3 52.1 all-gather.4
  64.1 99.5 all-gather.2
  388.1 87.7 reduce-scatter.3
where the time goes:
time: 494 us; the launch traced here: 485 us
  matrix products  156 us (32%)
  waiting for transfers between devices  151 us (31%)
  local copies, waits for them, and re-layouts  98.8 us (20%)
  other arithmetic  40.3 us (8%)
  starting transfers between devices  23.8 us (5%)
  between operations  14.3 us (3%)
    all_gather x1, waiting for transfers between devices, per_device(): cot_all = lax.all_gather(out_grad, 'seq', axis=0, tiled=True)  83.5 us
    dot_general x25, matrix products, multiply(): return jnp.einsum(pattern, left, right, preferred_element_type=jnp.float32)  57.5 us
    dot_general x5, matrix products, tile_attention(): jnp.einsum('anb,antd->btd', owners, grad_key_near.reshape(tile_count, nei...  36.3 us
    dot_general x5, matrix products, tile_attention(): jnp.einsum('anb,antd->btd', owners, grad_value_near.reshape(tile_count, n...  25.7 us
    unnamed x56, local copies, waits for them, and re-layouts  24 us
    select_n x5, other arithmetic, tile_attention(): jnp.take(key_tiles, tile_pairs, axis=0)  20.2 us
    unnamed x4, waiting for transfers between devices  18 us
    all_to_all x1, waiting for transfers between devices, per_device(): lax.all_to_all(key_normed, 'seq', split_axis=1, concat_axis=0, tiled=True)  14.4 us
  transfers between devices with their start and end apart: 9, of which 8 were waited for; matrix products, arithmetic and copies ran while one was open for 12% of the time, Pallas kernels for 0%

commit v1 on v0

--- a/solution.py
+++ b/solution.py
@@ -85,7 +85,9 @@
         lax.all_to_all(key_normed, "seq", split_axis=1, concat_axis=0, tiled=True),
         lax.all_to_all(values, "seq", split_axis=1, concat_axis=0, tiled=True),
     )
-    cot_all = lax.all_gather(out_grad, "seq", axis=0, tiled=True)
+    cot_all = jnp.concatenate(
+        lax.all_to_all(jnp.stack([out_grad] * lax.axis_size("seq")), "seq", 0, 0), axis=0
+    )
     columns = cot_all
     grad_attended = jnp.dot(
         columns, lax.all_gather(w_out, "dp", axis=0, tiled=True), preferred_element_type=jnp.float32

time: 494 us -> 533 us (1.079)
  blocking collectives: 0 us -> 20.4 us
  local copies, waits for them, and re-layouts: 98.8 us -> 107 us
  waiting for transfers between devices: 151 us -> 157 us
    all_to_all x1, waiting for transfers between devices: 8.08 us -> 101 us  [per_device(): lax.all_to_all(jnp.stack([out_grad] * lax.axis_size('seq')), 'seq', 0, 0)]
    all_gather x1 -> x0, waiting for transfers between devices: 83.5 us -> none  [per_device(): cot_all = lax.all_gather(out_grad, 'seq', axis=0, tiled=True)]
    all_to_all x0 -> x1, blocking collectives: none -> 20.4 us  [per_device(): lax.all_to_all(values, 'seq', split_axis=1, concat_axis=0, tiled=True)]
    unnamed x4 -> x3, waiting for transfers between devices: 18 us -> 26.5 us
    another operation x5 -> x6, local copies, waits for them, and re-layouts: 0.34 us -> 7.24 us  [the longest x1 6.9 us: per_device(): jnp.stack([out_grad] * lax.axis_size('seq'))]
    unnamed x56 -> x54, local copies, waits for them, and re-layouts: 24 us -> 25.2 us
  transfers between devices with their start and end apart: 9 -> 8, of which waited for: 8 -> 5; matrix products, arithmetic and copies ran while one was open for 12% -> 13% of each run, Pallas kernels for 0% -> 0%
where the time goes in v1:
time: 533 us; the launch traced here: 523 us
  waiting for transfers between devices  157 us (29%)
  matrix products  156 us (29%)
  local copies, waits for them, and re-layouts  107 us (20%)
  other arithmetic  40.3 us (8%)
  starting transfers between devices  26.4 us (5%)
  blocking collectives  20.4 us (4%)
  between operations  14.8 us (3%)
    all_to_all x1, waiting for transfers between devices, per_device(): lax.all_to_all(jnp.stack([out_grad] * lax.axis_size('seq')), 'seq', 0, 0)  101 us
    dot_general x25, matrix products, multiply(): return jnp.einsum(pattern, left, right, preferred_element_type=jnp.float32)  57.6 us
    dot_general x5, matrix products, tile_attention(): jnp.einsum('anb,antd->btd', owners, grad_key_near.reshape(tile_count, nei...  36.3 us
    unnamed x3, waiting for transfers between devices  26.5 us
    dot_general x5, matrix products, tile_attention(): jnp.einsum('anb,antd->btd', owners, grad_value_near.reshape(tile_count, n...  25.7 us
    unnamed x54, local copies, waits for them, and re-layouts  25.2 us
    all_to_all x1, blocking collectives, per_device(): lax.all_to_all(values, 'seq', split_axis=1, concat_axis=0, tiled=True)  20.4 us
    select_n x5, other arithmetic, tile_attention(): jnp.take(key_tiles, tile_pairs, axis=0)  20.1 us
  transfers between devices with their start and end apart: 8, of which 5 were waited for; matrix products, arithmetic and copies ran while one was open for 13% of the time, Pallas kernels for 0%

profile of v1, /device:TPU:0, one launch (start us, length us, event | category | flops | bytes accessed | tf_op | source)
XLA Modules:
  0.0 522.8 jit_solution(1043384552491140459)
XLA Ops:
  12.5 4.5 all-to-all-start
  21.1 2.5 copy.75
  23.6 11.4 %all-to-all-done = bf16[256,4,640]{2,0,1:T(8,128)(2,1)S(1)} async-done(((bf16[256,4,640]{2,0,1:T(8,128)(2,1)}), bf16[256,4,640]{2,0,1:T(8,128)(2,1)S(1)}, u32[]{:S(2)}, u32[]{:S(2)}) %all-to-all-start) | async-done | bytes 1310752 | tf_op jit(solution)/shard_map/all_to_all | solution.py:84
  34.9 3.5 all-to-all-start.1
  38.5 2.5 copy.126
  41.0 14.5 %all-to-all-done.1 = bf16[256,4,640]{2,0,1:T(8,128)(2,1)S(1)} async-done(((bf16[256,4,640]{2,0,1:T(8,128)(2,1)}), bf16[256,4,640]{2,0,1:T(8,128)(2,1)S(1)}, u32[]{:S(2)}, u32[]{:S(2)}) %all-to-all-start.1) | async-done | bytes 1310752 | tf_op jit(solution)/shard_map/all_to_all | solution.py:85
  55.5 20.4 %all_to_all.98 = bf16[256,4,640]{2,0,1:T(8,128)(2,1)} all-to-all(bf16[256,4,640]{2,0,1:T(8,128)(2,1)} %bitcast.189), channel_id=1, replica_groups=mesh['dp'=32,'seq'=4] {'seq'}, dimensions={1} | all-to-all | bytes 2621440 | tf_op jit(solution)/shard_map/all_to_all | solution.py:86
  75.9 6.9 %stack.2 = bf16[4,256,5120]{2,1,0:T(8,128)(2,1)} broadcast(bf16[256,5120]{1,0:T(8,128)(2,1)} %param.20), dimensions={1,2} | broadcast | bytes 13107200 | tf_op jit(solution)/shard_map/stack | solution.py:89
  82.8 6.1 %all-to-all-start.3 = ((bf16[4,256,5120]{2,1,0:T(8,128)(2,1)}), bf16[4,256,5120]{2,1,0:T(8,128)(2,1)}, u32[]{:S(2)}, u32[]{:S(2)}) async-start(bf16[4,256,5120]{2,1,0:T(8,128)(2,1)} %stack.2), calls=%async_computation.3 | async-start | bytes 20971520 | tf_op jit(solution)/shard_map/all_to_all | solution.py:89
  92.4 3.1 reshape.164
  97.0 3.1 reshape.165
  101.5 100.6 %all-to-all-done.3 = bf16[4,256,5120]{2,1,0:T(8,128)(2,1)} async-done(((bf16[4,256,5120]{2,1,0:T(8,128)(2,1)}), bf16[4,256,5120]{2,1,0:T(8,128)(2,1)}, u32[]{:S(2)}, u32[]{:S(2)}) %all-to-all-start.3) | async-done | bytes 10485792 | tf_op jit(solution)/shard_map/all_to_all | solution.py:89
  202.1 13.7 %convolution_convert_fusion.1 = bf16[1024,640]{1,0:T(8,128)(2,1)} fusion(bf16[1024,5120]{1,0:T(8,128)(2,1)} %bitcast.28, bf16[5120,640]{1,0:T(8,128)(2,1)} %all-gather.2.cloned.1.call-done), kind=kOutput, calls=%fused_computation.95 | convolution fusion | flops 6711541760 | bytes 18350080 | tf_op jit(solution)/shard_map/dot_general | solution.py:92
  215.8 3.1 reshape.167
  220.3 182.3 %while.18 = (s32[]{:T(128)}, bf16[5,16,64,128]{3,2,1,0:T(8,128)(2,1)}, bf16[5,16,64,128]{3,2,1,0:T(8,128)(2,1)}, bf16[5,16,64,128]{3,1,2,0:T(8,128)(2,1)}, bf16[...) while((s32[]{:T(128)}, ...), condition=%wide.region_6.8_spmd, body=%wide.region_2.7_spmd.sunk | while | flops 1219638656 | bytes 88276472 | solution.py:105
  225.9 4.0 broadcast_select_fusion.6
  232.5 3.6 fusion.136
  239.6 2.8 convolution_multiply_fusion.3
  242.5 7.2 %fusion.138 = bf16[5,16,64,128]{3,1,2,0:T(8,128)(2,1)} fusion(bf16[5,16,64,128]{3,1,2,0:T(8,128)(2,1)} %get-tuple-element.341, s32[]{:T(128)S(6)} %copy.142, f32[16,8,64,128]{3,2,1,0:T(8,128)} %bitcast.173, s32[16,8]{0,1:T(8,128)S(1)} %copy.132), kind=kOutput, calls=%fused_computation.26.clone.1 | convolution fusion | flops 201459712 | bytes 4456964 | tf_op jit(solution)/shard_map/while/body/eval_jaxpr/anb,antd->btd/dot_general | solution.py:55
  251.7 5.1 fusion.140
  262.3 4.0 broadcast_select_fusion.6
  266.6 2.3 fusion.135
  268.9 3.6 fusion.136
  276.0 2.8 convolution_multiply_fusion.3
  278.9 7.3 %fusion.138 = bf16[5,16,64,128]{3,1,2,0:T(8,128)(2,1)} fusion(bf16[5,16,64,128]{3,1,2,0:T(8,128)(2,1)} %get-tuple-element.341, s32[]{:T(128)S(6)} %copy.142, f32[16,8,64,128]{3,2,1,0:T(8,128)} %bitcast.173, s32[16,8]{0,1:T(8,128)S(1)} %copy.132), kind=kOutput, calls=%fused_computation.26.clone.1 | convolution fusion | flops 201459712 | bytes 4456964 | tf_op jit(solution)/shard_map/while/body/eval_jaxpr/anb,antd->btd/dot_general | solution.py:55
  288.1 5.1 fusion.140
  298.7 4.0 broadcast_select_fusion.6
  305.2 3.6 fusion.136
  312.4 2.8 convolution_multiply_fusion.3
  315.3 7.3 %fusion.138 = bf16[5,16,64,128]{3,1,2,0:T(8,128)(2,1)} fusion(bf16[5,16,64,128]{3,1,2,0:T(8,128)(2,1)} %get-tuple-element.341, s32[]{:T(128)S(6)} %copy.142, f32[16,8,64,128]{3,2,1,0:T(8,128)} %bitcast.173, s32[16,8]{0,1:T(8,128)S(1)} %copy.132), kind=kOutput, calls=%fused_computation.26.clone.1 | convolution fusion | flops 201459712 | bytes 4456964 | tf_op jit(solution)/shard_map/while/body/eval_jaxpr/anb,antd->btd/dot_general | solution.py:55
  324.5 5.1 fusion.140
  335.1 4.0 broadcast_select_fusion.6
  339.3 2.3 fusion.135
  341.6 3.6 fusion.136
  348.8 2.8 convolution_multiply_fusion.3
  351.7 7.3 %fusion.138 = bf16[5,16,64,128]{3,1,2,0:T(8,128)(2,1)} fusion(bf16[5,16,64,128]{3,1,2,0:T(8,128)(2,1)} %get-tuple-element.341, s32[]{:T(128)S(6)} %copy.142, f32[16,8,64,128]{3,2,1,0:T(8,128)} %bitcast.173, s32[16,8]{0,1:T(8,128)S(1)} %copy.132), kind=kOutput, calls=%fused_computation.26.clone.1 | convolution fusion | flops 201459712 | bytes 4456964 | tf_op jit(solution)/shard_map/while/body/eval_jaxpr/anb,antd->btd/dot_general | solution.py:55
  360.9 5.1 fusion.140
  371.4 4.0 broadcast_select_fusion.6
  375.7 2.3 fusion.135
  378.0 3.6 fusion.136
  385.1 2.8 convolution_multiply_fusion.3
  388.1 7.3 %fusion.138 = bf16[5,16,64,128]{3,1,2,0:T(8,128)(2,1)} fusion(bf16[5,16,64,128]{3,1,2,0:T(8,128)(2,1)} %get-tuple-element.341, s32[]{:T(128)S(6)} %copy.142, f32[16,8,64,128]{3,2,1,0:T(8,128)} %bitcast.173, s32[16,8]{0,1:T(8,128)S(1)} %copy.132), kind=kOutput, calls=%fused_computation.26.clone.1 | convolution fusion | flops 201459712 | bytes 4456964 | tf_op jit(solution)/shard_map/while/body/eval_jaxpr/anb,antd->btd/dot_general | solution.py:55
  397.3 5.2 fusion.140
  402.6 2.4 copy.90
  405.0 11.5 %fusion.68 = bf16[5120,640]{0,1:T(8,128)(2,1)} fusion(bf16[1024,5120]{1,0:T(8,128)(2,1)} %bitcast.28, bf16[128,8,5,128]{3,2,1,0:T(8,128)(2,1)S(1)} %bitcast.193), kind=kOutput, calls=%fused_computation.66 | convolution fusion | flops 6717440000 | bytes 18350080 | tf_op jit(solution)/shard_map/td,te->de/dot_general | solution.py:115
  416.6 9.5 %copy.97 = bf16[5120,640]{1,0:T(8,128)(2,1)} copy(bf16[5120,640]{0,1:T(8,128)(2,1)} %fusion.68) | data formatting | bytes 13107200
  428.4 2.4 all_to_all.83
  430.8 3.5 all-to-all-start.4
  434.4 2.3 copy.86
  436.7 2.5 all_to_all.85
  439.1 2.3 copy.88
  441.5 2.5 all_to_all.87
  443.9 4.3 all-to-all-done.4
  449.3 3.8 all-to-all-start.5
  453.1 3.1 convert_bitcast_fusion.1
  456.2 3.4 copy.85
  459.6 2.5 fusion.76
  464.1 2.4 copy.91
  467.6 4.8 all-to-all-start.6
  472.4 3.0 convert_bitcast_fusion
  475.3 3.4 copy.87
  478.8 2.4 fusion.84
  483.1 2.4 copy.92
  487.7 25.8 %reduce-scatter.4.cloned.1.call-done = bf16[160,640]{1,0:T(8,128)(2,1)} async-done(((bf16[5120,640]{1,0:T(8,128)(2,1)}), bf16[160,640]{1,0:T(8,128)(2,1)}) %reduce-scatter.4.cloned.1.call-update) | async-done | bytes 204816
  (197 shorter events, 90.3 us)
Async XLA Ops:
  7.2 82.1 %copy-start = (s32[1,16]{1,0:T(1,128)S(1)}, s32[1,16]{1,0:T(1,128)}, u32[]{:S(2)}) copy-start(s32[1,16]{1,0:T(1,128)} %param.19) | copy-start | bytes 196
  7.2 3.3 copy-start.15
  7.2 194.9 %all-gather.2.cloned.1.call-start = ((), (), s32[]{:S(2)}) async-start(), calls=%async_computation.8 | async-start | bytes 6758400 | tf_op jit(solution)/shard_map/all_gather | solution.py:93
  9.5 3.0 copy-start.7
  10.5 0.5 copy-start.22
  12.5 22.5 %all-to-all-start = ((bf16[256,4,640]{2,0,1:T(8,128)(2,1)}), bf16[256,4,640]{2,0,1:T(8,128)(2,1)S(1)}, u32[]{:S(2)}, u32[]{:S(2)}) async-start(bf16[256,4,640]{2,0,1:T(8,128)(2,1)} %copy.73), calls=%async_computation | async-start | bytes 2621440 | tf_op jit(solution)/shard_map/all_to_all | solution.py:84
  17.0 2.6 copy-start.17
  18.7 4.9 copy-start.5
  19.6 3.9 copy-start.20
  34.9 20.5 %all-to-all-start.1 = ((bf16[256,4,640]{2,0,1:T(8,128)(2,1)}), bf16[256,4,640]{2,0,1:T(8,128)(2,1)S(1)}, u32[]{:S(2)}, u32[]{:S(2)}) async-start(bf16[256,4,640]{2,0,1:T(8,128)(2,1)} %copy.75), calls=%async_computation.1 | async-start | bytes 2621440 | tf_op jit(solution)/shard_map/all_to_all | solution.py:85
  55.5 27.3 %copy-start.11 = (bf16[256,4,640]{2,0,1:T(8,128)(2,1)}, bf16[256,4,640]{2,0,1:T(8,128)(2,1)S(1)}, u32[]{:S(2)}) copy-start(bf16[256,4,640]{2,0,1:T(8,128)(2,1)S(1)} %all-to-all-done.1) | copy-start | bytes 3932164
  82.8 6.2 %copy-start.19 = (s32[16,8]{0,1:T(8,128)S(1)}, s32[16,8]{0,1:T(8,128)}, u32[]{:S(2)}) copy-start(s32[16,8]{0,1:T(8,128)} %param.18) | copy-start | bytes 1540
  82.8 119.3 %all-to-all-start.3 = ((bf16[4,256,5120]{2,1,0:T(8,128)(2,1)}), bf16[4,256,5120]{2,1,0:T(8,128)(2,1)}, u32[]{:S(2)}, u32[]{:S(2)}) async-start(bf16[4,256,5120]{2,1,0:T(8,128)(2,1)} %stack.2), calls=%async_computation.3 | async-start | bytes 20971520 | tf_op jit(solution)/shard_map/all_to_all | solution.py:89
  88.9 424.6 %reduce-scatter.4.cloned.1.call-start = ((), (), s32[]{:S(2)}) async-start(), calls=%async_computation.9 | async-start | bytes 6758400
  232.5 3.6 copy-start.2
  232.5 3.6 copy-start.3
  242.5 7.3 %copy-start.4 = (f32[16,64,512]{2,1,0:T(8,128)S(1)}, f32[16,64,512]{2,1,0:T(8,128)}, u32[]{:S(2)}) copy-start(f32[16,64,512]{2,1,0:T(8,128)} %get-tuple-element.322) | copy-start | bytes 6291460 | tf_op jit(solution)/shard_map/while
  268.9 3.6 copy-start.2
  268.9 3.6 copy-start.3
  278.9 7.3 %copy-start.4 = (f32[16,64,512]{2,1,0:T(8,128)S(1)}, f32[16,64,512]{2,1,0:T(8,128)}, u32[]{:S(2)}) copy-start(f32[16,64,512]{2,1,0:T(8,128)} %get-tuple-element.322) | copy-start | bytes 6291460 | tf_op jit(solution)/shard_map/while
  305.2 3.6 copy-start.2
  305.2 3.6 copy-start.3
  315.3 7.3 %copy-start.4 = (f32[16,64,512]{2,1,0:T(8,128)S(1)}, f32[16,64,512]{2,1,0:T(8,128)}, u32[]{:S(2)}) copy-start(f32[16,64,512]{2,1,0:T(8,128)} %get-tuple-element.322) | copy-start | bytes 6291460 | tf_op jit(solution)/shard_map/while
  341.6 3.6 copy-start.2
  341.6 3.6 copy-start.3
  351.7 7.3 %copy-start.4 = (f32[16,64,512]{2,1,0:T(8,128)S(1)}, f32[16,64,512]{2,1,0:T(8,128)}, u32[]{:S(2)}) copy-start(f32[16,64,512]{2,1,0:T(8,128)} %get-tuple-element.322) | copy-start | bytes 6291460 | tf_op jit(solution)/shard_map/while
  378.0 3.6 copy-start.2
  378.0 3.6 copy-start.3
  388.1 7.3 %copy-start.4 = (f32[16,64,512]{2,1,0:T(8,128)S(1)}, f32[16,64,512]{2,1,0:T(8,128)}, u32[]{:S(2)}) copy-start(f32[16,64,512]{2,1,0:T(8,128)} %get-tuple-element.322) | copy-start | bytes 6291460 | tf_op jit(solution)/shard_map/while
  426.0 1.3 copy-start.14
  430.8 17.4 %all-to-all-start.4 = ((bf16[4,256,640]{2,1,0:T(8,128)(2,1)}), bf16[4,256,640]{2,1,0:T(8,128)(2,1)S(1)}, u32[]{:S(2)}, u32[]{:S(2)}) async-start(bf16[4,256,640]{2,1,0:T(8,128)(2,1)} %all_to_all.83), calls=%async_computation.4 | async-start | bytes 2621440 | tf_op jit(solution)/shard_map/all_to_all | solution.py:123
  448.2 1.1 copy-start.13
  449.3 17.3 %all-to-all-start.5 = ((bf16[4,256,640]{2,1,0:T(8,128)(2,1)}), bf16[4,256,640]{2,1,0:T(8,128)(2,1)S(1)}, u32[]{:S(2)}, u32[]{:S(2)}) async-start(bf16[4,256,640]{2,1,0:T(8,128)(2,1)} %all_to_all.85), calls=%async_computation.5 | async-start | bytes 2621440 | tf_op jit(solution)/shard_map/all_to_all | solution.py:124
  456.2 3.4 copy-start.8
  456.2 3.4 copy-start.16
  459.6 2.8 copy-start.9
  459.6 2.7 copy-start.23
  459.6 2.7 copy-start.25
  466.6 1.1 copy-start.12
  467.6 17.9 %all-to-all-start.6 = ((bf16[4,256,640]{2,1,0:T(8,128)(2,1)}), bf16[4,256,640]{2,1,0:T(8,128)(2,1)S(1)}, u32[]{:S(2)}, u32[]{:S(2)}) async-start(bf16[4,256,640]{2,1,0:T(8,128)(2,1)} %all_to_all.87), calls=%async_computation.6 | async-start | bytes 2621440 | tf_op jit(solution)/shard_map/all_to_all | solution.py:125
  475.3 3.4 copy-start.6
  475.3 3.4 copy-start.18
  478.7 2.6 copy-start.10
  478.7 2.6 copy-start.21
  478.8 2.6 copy-start.24
  485.5 30.0 %copy-start.1 = (s32[1,16]{1,0:T(1,128)S(1)}, s32[1,16]{1,0:T(1,128)}, u32[]{:S(2)}) copy-start(s32[1,16]{1,0:T(1,128)} %param.19) | copy-start | bytes 196
Sparse Core Ops, SparseCore 0:
  10.3 52.1 all-gather.1
  426.2 87.2 reduce-scatter.3
